TPU v7x, 32 devices: a whole 2x2x4 slice. The times are simulated.
32 devices in a mesh: dp: 16 (over z, x, core), mp: 2 (over y).
Axes of the slice: x: 2, y: 2, z: 4, core: 2. Of those that a mesh axis runs over, the one named last changes fastest.
Arguments:
- tokens: bfloat16 [16384, 1024], P('dp'), may hold values from -6 to 6
- page_lengths: int32 [32], P('dp'), may hold values from 64 to 512, as said below
- qkv_weight: bfloat16 [3, 1024, 1024], P(None, None, 'mp'), may hold values from -0.1875 to 0.1875
- qv_bias: bfloat16 [2, 1024], P(None, 'mp'), may hold values from -1.5 to 1.5
- out_weight: bfloat16 [1024, 1024], P('mp'), may hold values from -0.75 to 0.75
- out_bias: bfloat16 [1024], replicated, may hold values from -1.5 to 1.5
- ln1_gain: bfloat16 [1024], replicated, may hold values from 0.5 to 1.5
- ln1_bias: bfloat16 [1024], replicated, may hold values from -1.5 to 1.5
- ff1_weight: bfloat16 [1024, 4096], P(None, 'mp'), may hold values from -0.1875 to 0.1875
- ff1_bias: bfloat16 [4096], P('mp'), may hold values from -1.5 to 1.5
- ff2_weight: bfloat16 [4096, 1024], P('mp'), may hold values from -0.09375 to 0.09375
- ff2_bias: bfloat16 [1024], replicated, may hold values from -1.5 to 1.5
- ln2_gain: bfloat16 [1024], replicated, may hold values from 0.5 to 1.5
- ln2_bias: bfloat16 [1024], replicated, may hold values from -1.5 to 1.5
- cotangent: bfloat16 [16384, 1024], P('dp'), may hold values from -6 to 6
Outputs:
- out_rows: bfloat16 [16384, 1024], P(('dp', 'mp'))
- input_grad: bfloat16 [16384, 1024], P(('dp', 'mp'))
- qkv_weight_grad: float32 [3, 1024, 1024], P(None, 'dp', 'mp')
- qv_bias_grad: float32 [2, 1024], replicated
- out_weight_grad: float32 [1024, 1024], P('mp', 'dp')
- out_bias_grad: float32 [1024], replicated
- ln1_gain_grad: float32 [1024], replicated
- ln1_bias_grad: float32 [1024], replicated
- ff1_weight_grad: float32 [1024, 4096], P('dp', 'mp')
- ff1_bias_grad: float32 [4096], replicated
- ff2_weight_grad: float32 [4096, 1024], P('mp', 'dp')
- ff2_bias_grad: float32 [1024], replicated
- ln2_gain_grad: float32 [1024], replicated
- ln2_bias_grad: float32 [1024], replicated
Inputs may be any that keep to these rules, and one draw needn't show every extreme that they name: `page_lengths`: valid tokens of a page; some page has all 512 slots valid.
All inputs are finite; a program needn't handle non-finite values.
Results may differ from a plain program's by a relative error of at most 0.02.
Values may be sent and summed in bfloat16 or wider, within the bound.
No kernel may reach another device: no remote copies, remote signals or barrier semaphores. Data moves between devices by JAX's collectives and lax.ppermute only.
A program may use at most 192 MiB of HBM per device.

v0:
```python
import jax
import jax.numpy as jnp
from jax import lax
from jax.sharding import PartitionSpec as P

HD = 64
EPSILON = 1e-05
NEGATIVE = -1e30


def normalize(values):
    center = values - jnp.mean(values, axis=-1, keepdims=True)
    spread = jnp.mean(center * center, axis=-1, keepdims=True)
    return center * lax.rsqrt(spread + EPSILON)


def gelu_exact(values):
    return jax.nn.gelu(values, approximate=False)


def over_rows(left, right):
    return lax.dot_general(
        left, right, (((0,), (0,)), ((), ())), preferred_element_type=jnp.float32
    )


def over_cols(left, right):
    return lax.dot_general(
        left, right, (((1,), (1,)), ((), ())), preferred_element_type=jnp.float32
    )


def page_scores(query, keyset, valid):
    raw = jnp.einsum("qhe,khe->hqk", query, keyset, preferred_element_type=jnp.float32) * HD ** (
        -0.5
    )
    return jnp.where(valid[None, None, :], raw, NEGATIVE)


def attend(block):
    query, keyset, valueset, valid = block
    scores = page_scores(query, keyset, valid)
    top = jnp.max(scores, axis=-1, keepdims=True)
    expo = jnp.exp(scores - top)
    total = jnp.sum(expo, axis=-1, keepdims=True)
    probs = expo / total
    context = jnp.einsum(
        "hqk,khe->qhe", probs.astype(jnp.bfloat16), valueset, preferred_element_type=jnp.float32
    )
    context = context.astype(jnp.bfloat16)
    return (context.reshape(context.shape[0], -1), top[..., 0] + jnp.log(total[..., 0]))


def attend_back(block):
    query, keyset, valueset, valid, logsum, dcontext = block
    scale = HD ** (-0.5)
    scores = page_scores(query, keyset, valid)
    probs = jnp.exp(scores - logsum[..., None])
    dprobs = jnp.einsum("qhe,khe->hqk", dcontext, valueset, preferred_element_type=jnp.float32)
    delta = jnp.sum(probs * dprobs, axis=-1, keepdims=True)
    dscores = (probs * (dprobs - delta)).astype(jnp.bfloat16)
    dquery = (
        jnp.einsum("hqk,khe->qhe", dscores, keyset, preferred_element_type=jnp.float32) * scale
    ).astype(jnp.bfloat16)
    dkeys = (
        jnp.einsum("hqk,qhe->khe", dscores, query, preferred_element_type=jnp.float32) * scale
    ).astype(jnp.bfloat16)
    dvalues = jnp.einsum(
        "hqk,qhe->khe", probs.astype(jnp.bfloat16), dcontext, preferred_element_type=jnp.float32
    ).astype(jnp.bfloat16)
    seq_len = query.shape[0]
    return (dquery.reshape(seq_len, -1), dkeys.reshape(seq_len, -1), dvalues.reshape(seq_len, -1))


def local(
    tokens,
    page_lengths,
    qkv_weight,
    qv_bias,
    out_weight,
    out_bias,
    ln1_gain,
    ln1_bias,
    ff1_weight,
    ff1_bias,
    ff2_weight,
    ff2_bias,
    ln2_gain,
    ln2_bias,
    cotangent,
):
    row_count = tokens.shape[0]
    page_count = page_lengths.shape[0]
    seq_len = row_count // page_count
    cols = qkv_weight.shape[2]
    ff_cols = ff1_weight.shape[1]
    group_heads = cols // HD
    share = row_count // lax.axis_size("mp")
    group = lax.axis_index("mp")
    share_start = group * share
    gain_one = ln1_gain.astype(jnp.float32)
    shift_one = ln1_bias.astype(jnp.float32)
    gain_two = ln2_gain.astype(jnp.float32)
    shift_two = ln2_bias.astype(jnp.float32)

    def own_rows(values):
        return lax.dynamic_slice_in_dim(values, share_start, share, 0)

    projected = jnp.einsum("rd,tdc->trc", tokens, qkv_weight, preferred_element_type=jnp.float32)
    bias_rows = jnp.stack([qv_bias[0], jnp.zeros_like(qv_bias[0]), qv_bias[1]]).astype(jnp.float32)
    qkv_rows = (projected + bias_rows[:, None, :]).astype(jnp.bfloat16)
    qkv_pages = qkv_rows.reshape(3, page_count, seq_len, group_heads, HD)
    valid = jnp.arange(seq_len)[None, :] < page_lengths[:, None]
    context, logsum = lax.map(attend, (qkv_pages[0], qkv_pages[1], qkv_pages[2], valid))
    context = context.reshape(row_count, cols)
    attn_part = jnp.dot(context, out_weight, preferred_element_type=jnp.float32).astype(
        jnp.bfloat16
    )
    attn = lax.psum(attn_part, "mp").astype(jnp.float32)
    first_sum = tokens.astype(jnp.float32) + attn + out_bias.astype(jnp.float32)
    normed_one, norm_one_back = jax.vjp(normalize, first_sum)
    hidden = normed_one * gain_one + shift_one
    hidden_low = hidden.astype(jnp.bfloat16)
    normed_one_own = own_rows(normed_one)
    pre = jnp.dot(hidden_low, ff1_weight, preferred_element_type=jnp.float32) + ff1_bias.astype(
        jnp.float32
    )
    activated, gelu_back = jax.vjp(gelu_exact, pre)
    act_low = activated.astype(jnp.bfloat16)
    ffn_part = jnp.dot(act_low, ff2_weight, preferred_element_type=jnp.float32).astype(jnp.bfloat16)
    cot_own = own_rows(cotangent).astype(jnp.float32)
    ffn = lax.psum(ffn_part, "mp").astype(jnp.float32)
    second_sum = hidden + ffn + ff2_bias.astype(jnp.float32)
    normed_two, norm_two_back = jax.vjp(normalize, second_sum)
    normed_two_own = own_rows(normed_two)
    out_rows = (normed_two_own * gain_two + shift_two).astype(jnp.bfloat16)
    dsecond = norm_two_back(cotangent.astype(jnp.float32) * gain_two)[0]
    dffn = dsecond.astype(jnp.bfloat16)
    dsecond_own = own_rows(dsecond)
    dgain_two = jnp.sum(cot_own * normed_two_own, axis=0)
    dshift_two = jnp.sum(cot_own, axis=0)
    dff2_bias = jnp.sum(dsecond_own, axis=0)
    dff2_weight = over_rows(act_low, dffn)
    dact = over_cols(dffn, ff2_weight)
    dpre = gelu_back(dact)[0].astype(jnp.bfloat16)
    dff1_bias = jnp.sum(dpre.astype(jnp.float32), axis=0)
    dff1_weight = over_rows(hidden_low, dpre)
    dhid_part = over_cols(dpre, ff1_weight).astype(jnp.bfloat16)
    dhidden = dsecond + lax.psum(dhid_part, "mp").astype(jnp.float32)
    dfirst = norm_one_back(dhidden * gain_one)[0]
    dattn = dfirst.astype(jnp.bfloat16)
    dhidden_own = own_rows(dhidden)
    dfirst_own = own_rows(dfirst)
    dgain_one = jnp.sum(dhidden_own * normed_one_own, axis=0)
    dshift_one = jnp.sum(dhidden_own, axis=0)
    dout_bias = jnp.sum(dfirst_own, axis=0)
    dout_weight = over_rows(context, dattn)
    dcontext = over_cols(dattn, out_weight).astype(jnp.bfloat16)
    dcontext_pages = dcontext.reshape(page_count, seq_len, group_heads, HD)
    dquery, dkeys, dvalues = lax.map(
        attend_back, (qkv_pages[0], qkv_pages[1], qkv_pages[2], valid, logsum, dcontext_pages)
    )
    dqkv = jnp.stack(
        [
            dquery.reshape(row_count, cols),
            dkeys.reshape(row_count, cols),
            dvalues.reshape(row_count, cols),
        ]
    )
    dqv_bias = jnp.stack(
        [jnp.sum(dqkv[0].astype(jnp.float32), axis=0), jnp.sum(dqkv[2].astype(jnp.float32), axis=0)]
    )
    dqkv_weight = jnp.einsum("rd,trc->tdc", tokens, dqkv, preferred_element_type=jnp.float32)
    dtok_part = jnp.einsum(
        "trc,tdc->rd", dqkv, qkv_weight, preferred_element_type=jnp.float32
    ).astype(jnp.bfloat16)
    input_grad = (
        dfirst_own
        + lax.psum_scatter(dtok_part, "mp", scatter_dimension=0, tiled=True).astype(jnp.float32)
    ).astype(jnp.bfloat16)
    qkv_share, out_share, ff1_share, ff2_share = (
        lax.psum_scatter(
            dqkv_weight.astype(jnp.bfloat16), "dp", scatter_dimension=1, tiled=True
        ).astype(jnp.float32),
        lax.psum_scatter(
            dout_weight.astype(jnp.bfloat16), "dp", scatter_dimension=1, tiled=True
        ).astype(jnp.float32),
        lax.psum_scatter(
            dff1_weight.astype(jnp.bfloat16), "dp", scatter_dimension=0, tiled=True
        ).astype(jnp.float32),
        lax.psum_scatter(
            dff2_weight.astype(jnp.bfloat16), "dp", scatter_dimension=1, tiled=True
        ).astype(jnp.float32),
    )
    qv_placed = lax.dynamic_update_slice_in_dim(
        jnp.zeros((2, cols * lax.axis_size("mp")), jnp.float32), dqv_bias, group * cols, 1
    )
    ff1_placed = lax.dynamic_update_slice_in_dim(
        jnp.zeros((ff_cols * lax.axis_size("mp"),), jnp.float32), dff1_bias, group * ff_cols, 0
    )
    small = lax.psum(
        (qv_placed, dout_bias, dgain_one, dshift_one, ff1_placed, dff2_bias, dgain_two, dshift_two),
        ("dp", "mp"),
    )
    return (
        out_rows,
        input_grad,
        qkv_share,
        small[0],
        out_share,
        small[1],
        small[2],
        small[3],
        ff1_share,
        small[4],
        ff2_share,
        small[5],
        small[6],
        small[7],
    )


def solution(mesh):
    in_specs = (
        P("dp", None),
        P("dp"),
        P(None, None, "mp"),
        P(None, "mp"),
        P("mp", None),
        P(),
        P(),
        P(),
        P(None, "mp"),
        P("mp"),
        P("mp", None),
        P(),
        P(),
        P(),
        P("dp", None),
    )
    out_specs = (
        P(("dp", "mp"), None),
        P(("dp", "mp"), None),
        P(None, "dp", "mp"),
        P(),
        P("mp", "dp"),
        P(),
        P(),
        P(),
        P("dp", "mp"),
        P(),
        P("mp", "dp"),
        P(),
        P(),
        P(),
    )
    return jax.shard_map(local, mesh=mesh, in_specs=in_specs, out_specs=out_specs, check_vma=False)
```

profile of v0, /device:TPU:0, one launch (start us, length us, event | category | flops | bytes accessed | tf_op | source)
XLA Modules:
  0.0 775.8 jit_solution(8002461027185806768)
XLA Ops:
  9.1 5.5 fusion.56
  32.4 24.3 %while.26 = (s32[]{:T(128)}, bf16[2,512,512]{2,1,0:T(8,128)(2,1)}, f32[2,8,512]{2,1,0:T(8,128)S(1)}, bf16[2,512,8,64]{1,3,2,0:T(8,128)(2,1)}, pred[2,512]{1,0:T(...) while((s32[]{:T(128)}, bf16[2,512,512]{2,1,0:T(8,128)(2,1)}, ...), condition=%wide.region_3.4_spmd, body=%wide.region_0.3_spmd.sunk | while | flops 562294784 | bytes 33689224 | solution.py:114
  56.7 4.2 convolution_convert_fusion.4
  61.3 65.4 %all-reduce.7.cloned.1.call-done = bf16[1024,1024]{1,0:T(8,128)(2,1)} async-done(((bf16[1024,1024]{1,0:T(8,128)(2,1)}), bf16[1024,1024]{1,0:T(8,128)(2,1)}) %all-reduce.7.cloned.1.call-update) | async-done | bytes 2097168 | tf_op jit(solution)/shard_map/psum | solution.py:119
  133.5 24.4 %multiply_convert_fusion.1 = (bf16[1024,2048]{1,0:T(8,128)(2,1)S(1)}, f32[1024,2048]{1,0:T(8,128)}, f32[1024,2048]{1,0:T(8,128)}) fusion(f32[2048]{0:T(1024)S(1)} %convert_element_type.172, bf16[1024,2048]{1,0:T(8,128)(2,1)S(1)} %copy-done.36, f32[1024,1024]{1,0:T(8,128)S(1)} %broadcast_multiply_fusion, f32[1024]{0:T(1024)S(1)} %convert_element_type.170, ...), kind=kOutput, calls=%fused_computation.64 | convolution fusion | flops 4436525056 | bytes 29376512 | tf_op jit(solution)/shard_map/dot_general | solution.py:125
  159.9 5.7 convolution_convert_fusion.3
  166.2 62.6 %all-reduce.9.cloned.1.call-done = bf16[1024,1024]{1,0:T(8,128)(2,1)} async-done(((bf16[1024,1024]{1,0:T(8,128)(2,1)}), bf16[1024,1024]{1,0:T(8,128)(2,1)}) %all-reduce.9.cloned.1.call-update) | async-done | bytes 2097168 | tf_op jit(solution)/shard_map/psum | solution.py:132
  241.1 13.0 %convert_reduce_fusion = (f32[2048]{0:T(1024)}, bf16[1024,2048]{1,0:T(8,128)(2,1)}) fusion(f32[1024,2048]{1,0:T(8,128)} %get-tuple-element.258, bf16[2048,1024]{1,0:T(8,128)(2,1)S(1)} %copy-done.35, f32[1024,1024]{1,0:T(8,128)S(1)} %broadcast_add_fusion.1, f32[1024,2048]{1,0:T(8,128)} %get-tuple-element.275, f32[2048]{0:T(1024)S(1)} %convert_element_type.172), kind=kOutput, calls=%fused_computation.62 | convolution fusion | flops 4331665408 | bytes 29376512 | tf_op jit(solution)/shard_map/dot_general | solution.py:28
  254.1 8.0 %convolution_convert_fusion.2 = bf16[1024,1024]{1,0:T(8,128)(2,1)} fusion(bf16[1024,2048]{1,0:T(8,128)(2,1)} %get-tuple-element.277, bf16[1024,2048]{1,0:T(8,128)(2,1)S(1)} %copy-done.37), kind=kOutput, calls=%fused_computation.118 | convolution fusion | flops 4296015872 | bytes 10485760 | tf_op jit(solution)/shard_map/dot_general | solution.py:28
  262.2 63.0 %all-reduce.11.cloned.1.call-done = bf16[1024,1024]{1,0:T(8,128)(2,1)} async-done(((bf16[1024,1024]{1,0:T(8,128)(2,1)}), bf16[1024,1024]{1,0:T(8,128)(2,1)}) %all-reduce.11.cloned.1.call-update) | async-done | bytes 2097168 | tf_op jit(solution)/shard_map/psum | solution.py:149
  325.2 5.7 multiply_reduce_fusion.1
  346.2 42.9 %while.27 = (s32[]{:T(128)}, bf16[2,512,512]{1,2,0:T(8,128)(2,1)}, bf16[2,512,512]{2,1,0:T(8,128)(2,1)}, bf16[2,512,512]{1,2,0:T(8,128)(2,1)}, bf16[2,512,8,64]{...) while((s32[]{:T(128)}, bf16[2,512,512]{1,2,0:T(8,128)(2,1)}, ...), condition=%wide.region_17.18_spmd, body=%wide.region_15.17_spmd.sunk | while | flops 1374941184 | bytes 89248512 | solution.py:160
  393.7 7.7 convert_bitcast_fusion
  401.4 7.7 copy.83
  409.1 4.8 convolution_convert_fusion.5
  414.0 10.2 %convolution_convert_fusion = bf16[2048,1024]{0,1:T(8,128)(2,1)} fusion(bf16[1024,2048]{1,0:T(8,128)(2,1)} %copy-done.40, f32[1024,1024]{1,0:T(8,128)} %copy-done.11), kind=kOutput, calls=%fused_computation.91 | convolution fusion | flops 4298113024 | bytes 12582912 | tf_op jit(solution)/shard_map/dot_general | solution.py:22
  424.3 6.6 bitcast_convert_fusion
  431.3 10.2 %convolution_convert_fusion.1 = bf16[1024,2048]{1,0:T(8,128)(2,1)} fusion(bf16[1024,2048]{1,0:T(8,128)(2,1)} %get-tuple-element.277, f32[1024,1024]{1,0:T(8,128)} %copy-done.7, f32[1024]{0:T(1024)S(1)} %copy-done.25, f32[1024]{0:T(1024)S(1)} %convert_element_type.169), kind=kOutput, calls=%fused_computation.92 | convolution fusion | flops 4300210176 | bytes 12591104 | tf_op jit(solution)/shard_map/dot_general | solution.py:22
  452.0 68.8 %all-reduce.13.cloned.1.call-done = bf16[3,1024,512]{2,0,1:T(4,128)(2,1)} async-done(((bf16[3,1024,512]{2,0,1:T(4,128)(2,1)}), bf16[3,1024,512]{2,0,1:T(4,128)(2,1)}) %all-reduce.13.cloned.1.call-update) | async-done | bytes 3145744
  522.7 57.9 %reduce-scatter.7.cloned.1.call-done = bf16[512,64]{0,1:T(8,128)(2,1)} async-done(((bf16[512,1024]{0,1:T(8,128)(2,1)}), bf16[512,64]{0,1:T(8,128)(2,1)}) %reduce-scatter.7.cloned.1.call-update) | async-done | bytes 65552 | tf_op jit(solution)/shard_map/reduce_scatter | solution.py:185
  582.1 74.2 %reduce-scatter.11.cloned.1.call-done = bf16[2048,64]{0,1:T(8,128)(2,1)} async-done(((bf16[2048,1024]{0,1:T(8,128)(2,1)}), bf16[2048,64]{0,1:T(8,128)(2,1)}) %reduce-scatter.11.cloned.1.call-update) | async-done | bytes 262160 | tf_op jit(solution)/shard_map/reduce_scatter | solution.py:191
  658.1 31.3 %reduce-scatter.5.cloned.1.call-done = bf16[512,1024]{1,0:T(8,128)(2,1)} async-done(((bf16[1024,1024]{1,0:T(8,128)(2,1)}), bf16[512,1024]{1,0:T(8,128)(2,1)}) %reduce-scatter.5.cloned.1.call-update) | async-done | bytes 1048592 | tf_op jit(solution)/shard_map/reduce_scatter | solution.py:179
  692.6 40.9 %all-reduce.1 = (f32[2,1024]{1,0:T(2,128)}, f32[1024]{0:T(1024)}, f32[1024]{0:T(1024)}, f32[1024]{0:T(1024)}, f32[4096]{0:T(1024)}, /*index=5*/f32[1024]{0:T(1024)}, f32[1024]{0:T(1024)}, f32[1024]{0:T(1024)}) all-reduce(f32[2,1024]{1,0:T(2,128)S(1)} %maximum_dynamic-update-slice_fusion, ...), channel_id=1, replica_groups=mesh['dp'=16,'mp'=2] {'dp','mp'}, use_global_device_ids=true, to_apply=%region_22.23 | all-reduce | flops 12288 | bytes 98304 | tf_op jit(solution)/shard_map/psum | solution.py:201
  733.5 33.2 %reduce-scatter.9.cloned.1.call-done = bf16[64,2048]{1,0:T(8,128)(2,1)} async-done(((bf16[1024,2048]{1,0:T(8,128)(2,1)}), bf16[64,2048]{1,0:T(8,128)(2,1)}) %reduce-scatter.9.cloned.1.call-update) | async-done | bytes 262160 | tf_op jit(solution)/shard_map/reduce_scatter | solution.py:188
  (204 shorter events, 148.5 us)
Async XLA Ops:
  7.2 119.5 %all-reduce.7.cloned.1.call-start = ((), (), s32[]{:S(2)}) async-start(), calls=%async_computation.4 | async-start | bytes 4194304 | tf_op jit(solution)/shard_map/psum | solution.py:119
  56.7 4.6 copy-start.27
  60.9 167.8 %all-reduce.9.cloned.1.call-start = ((), (), s32[]{:S(2)}) async-start(), calls=%async_computation.5 | async-start | bytes 4194304 | tf_op jit(solution)/shard_map/psum | solution.py:132
  61.3 171.4 %copy-start.24 = (f32[1024]{0:T(1024)}, f32[1024]{0:T(1024)S(1)}, u32[]{:S(2)}) copy-start(f32[1024]{0:T(1024)S(1)} %convert_element_type.170) | copy-start | bytes 12292
  133.4 24.4 %copy-start.7 = (f32[1024,1024]{1,0:T(8,128)}, f32[1024,1024]{1,0:T(8,128)S(1)}, u32[]{:S(2)}) copy-start(f32[1024,1024]{1,0:T(8,128)S(1)} %broadcast_multiply_fusion) | copy-start | bytes 12582916
  133.5 26.5 %copy-start.34 = (bf16[2048,1024]{1,0:T(8,128)(2,1)S(1)}, bf16[2048,1024]{1,0:T(8,128)(2,1)}, u32[]{:S(2)}) copy-start(bf16[2048,1024]{1,0:T(8,128)(2,1)} %param.29) | copy-start | bytes 12582916
  159.9 6.2 copy-start.31
  159.9 6.2 copy-start.32
  165.7 159.5 %all-reduce.11.cloned.1.call-start = ((), (), s32[]{:S(2)}) async-start(), calls=%async_computation.6 | async-start | bytes 4194304 | tf_op jit(solution)/shard_map/psum | solution.py:149
  166.2 72.0 %copy-start.20 = (f32[1024]{0:T(1024)}, f32[1024]{0:T(1024)S(1)}, u32[]{:S(2)}) copy-start(f32[1024]{0:T(1024)S(1)} %convert_element_type.177) | copy-start | bytes 12292
  228.8 4.7 copy-start.13
  239.4 14.7 %copy-start.11 = (f32[1024,1024]{1,0:T(8,128)}, f32[1024,1024]{1,0:T(8,128)S(1)}, u32[]{:S(2)}) copy-start(f32[1024,1024]{1,0:T(8,128)S(1)} %broadcast_add_fusion.1) | copy-start | bytes 12582916
  241.1 13.0 %copy-start.37 = (bf16[1024,2048]{1,0:T(8,128)(2,1)S(1)}, bf16[1024,2048]{1,0:T(8,128)(2,1)}, u32[]{:S(2)}) copy-start(bf16[1024,2048]{1,0:T(8,128)(2,1)} %param.27) | copy-start | bytes 12582916
  262.1 258.7 %all-reduce.13.cloned.1.call-start = ((), (), s32[]{:S(2)}) async-start(), calls=%async_computation.11 | async-start | bytes 8388608
  325.2 5.8 copy-start.4
  325.2 5.8 copy-start.6
  409.1 171.5 %reduce-scatter.7.cloned.1.call-start = ((), (), s32[]{:S(2)}) async-start(), calls=%async_computation.8 | async-start | bytes 1114112 | tf_op jit(solution)/shard_map/reduce_scatter | solution.py:185
  414.0 242.3 %reduce-scatter.11.cloned.1.call-start = ((), (), s32[]{:S(2)}) async-start(), calls=%async_computation.10 | async-start | bytes 4456448 | tf_op jit(solution)/shard_map/reduce_scatter | solution.py:191
  424.3 7.0 copy-start.25
  424.3 265.1 %reduce-scatter.5.cloned.1.call-start = ((), (), s32[]{:S(2)}) async-start(), calls=%async_computation.7 | async-start | bytes 3145728 | tf_op jit(solution)/shard_map/reduce_scatter | solution.py:179
  431.0 335.8 %reduce-scatter.9.cloned.1.call-start = ((), (), s32[]{:S(2)}) async-start(), calls=%async_computation.9 | async-start | bytes 4456448 | tf_op jit(solution)/shard_map/reduce_scatter | solution.py:188
  443.4 6.0 copy-start.9
  445.8 5.8 copy-start.18
  445.8 5.8 copy-start.19
  (30 other events, 79.6 us)
Sparse Core Ops, SparseCore 0:
  61.1 65.5 all-reduce.6
  165.8 62.9 all-reduce.8
  262.2 62.9 all-reduce.10
  409.2 111.5 all-reduce.12
  524.3 56.2 reduce-scatter.6
  584.8 71.4 reduce-scatter.10
  658.5 30.8 reduce-scatter.4
  693.8 72.9 reduce-scatter.8
where the time goes:
time: 785 us; the launch traced here: 776 us
  waiting for transfers between devices  457 us (58%)
  matrix products  139 us (18%)
  local copies, waits for them, and re-layouts  70.2 us (9%)
  other arithmetic  51.3 us (7%)
  blocking collectives  40.9 us (5%)
  between operations  15.7 us (2%)
    reduce_scatter x1, waiting for transfers between devices, local(): lax.psum_scatter(dff2_weight.astype(jnp.bfloat16), 'dp', scatter_dimensio...  74.2 us
    unnamed x9, waiting for transfers between devices  68.9 us
    psum x1, waiting for transfers between devices, local(): attn = lax.psum(attn_part, 'mp').astype(jnp.float32)  65.4 us
    psum x1, waiting for transfers between devices, local(): dhidden = dsecond + lax.psum(dhid_part, 'mp').astype(jnp.float32)  63 us
    psum x1, waiting for transfers between devices, local(): ffn = lax.psum(ffn_part, 'mp').astype(jnp.float32)  62.6 us
    reduce_scatter x1, waiting for transfers between devices, local(): lax.psum_scatter(dout_weight.astype(jnp.bfloat16), 'dp', scatter_dimensio...  57.9 us
    psum x1, blocking collectives, local(): lax.psum((qv_placed, dout_bias, dgain_one, dshift_one, ff1_placed, dff2_b...  40.9 us
    reduce_scatter x1, waiting for transfers between devices, local(): lax.psum_scatter(dff1_weight.astype(jnp.bfloat16), 'dp', scatter_dimensio...  33.2 us
  transfers between devices with their start and end apart: 8, of which 8 were waited for; matrix products, arithmetic and copies ran while one was open for 6% of the time, Pallas kernels for 0%

commit v1 on v0

--- a/solution.py
+++ b/solution.py
@@ -146,7 +146,9 @@
     dff1_bias = jnp.sum(dpre.astype(jnp.float32), axis=0)
     dff1_weight = over_rows(hidden_low, dpre)
     dhid_part = over_cols(dpre, ff1_weight).astype(jnp.bfloat16)
-    dhidden = dsecond + lax.psum(dhid_part, "mp").astype(jnp.float32)
+    dhidden = dsecond + jnp.sum(jax.lax.all_gather(dhid_part, axis_name="mp"), 0).astype(
+        jnp.float32
+    )
     dfirst = norm_one_back(dhidden * gain_one)[0]
     dattn = dfirst.astype(jnp.bfloat16)
     dhidden_own = own_rows(dhidden)

time: 785 us -> 825 us (1.051)
  waiting for transfers between devices: 457 us -> 492 us
    psum x1 -> x0, waiting for transfers between devices: 63 us -> none  [local(): dhidden = dsecond + lax.psum(dhid_part, 'mp').astype(jnp.float32)]
    all_gather x0 -> x1, waiting for transfers between devices: none -> 56.9 us  [local(): jax.lax.all_gather(dhid_part, axis_name='mp')]
    reduce_scatter x1, waiting for transfers between devices: 33.2 us -> 74 us  [local(): lax.psum_scatter(dff1_weight.astype(jnp.bfloat16), 'dp', scatter_dimensio...]
where the time goes in v1:
time: 825 us; the launch traced here: 816 us
  waiting for transfers between devices  492 us (60%)
  matrix products  139 us (17%)
  local copies, waits for them, and re-layouts  69.9 us (8%)
  other arithmetic  56.4 us (7%)
  blocking collectives  40.7 us (5%)
  between operations  15.8 us (2%)
    reduce_scatter x1, waiting for transfers between devices, local(): lax.psum_scatter(dff1_weight.astype(jnp.bfloat16), 'dp', scatter_dimensio...  74 us
    reduce_scatter x1, waiting for transfers between devices, local(): lax.psum_scatter(dff2_weight.astype(jnp.bfloat16), 'dp', scatter_dimensio...  73.9 us
    unnamed x9, waiting for transfers between devices  69.2 us
    psum x1, waiting for transfers between devices, local(): attn = lax.psum(attn_part, 'mp').astype(jnp.float32)  65.4 us
    psum x1, waiting for transfers between devices, local(): ffn = lax.psum(ffn_part, 'mp').astype(jnp.float32)  62.6 us
    reduce_scatter x1, waiting for transfers between devices, local(): lax.psum_scatter(dout_weight.astype(jnp.bfloat16), 'dp', scatter_dimensio...  58.4 us
    all_gather x1, waiting for transfers between devices, local(): jax.lax.all_gather(dhid_part, axis_name='mp')  56.9 us
    psum x1, blocking collectives, local(): lax.psum((qv_placed, dout_bias, dgain_one, dshift_one, ff1_placed, dff2_b...  40.7 us
  transfers between devices with their start and end apart: 8, of which 8 were waited for; matrix products, arithmetic and copies ran while one was open for 6% of the time, Pallas kernels for 0%

profile of v1, /device:TPU:0, one launch (start us, length us, event | category | flops | bytes accessed | tf_op | source)
XLA Modules:
  0.0 815.7 jit_solution(12681454612687802865)
XLA Ops:
  9.1 5.5 fusion.56
  32.4 24.3 %while.26 = (s32[]{:T(128)}, bf16[2,512,512]{2,1,0:T(8,128)(2,1)}, f32[2,8,512]{2,1,0:T(8,128)S(1)}, bf16[2,512,8,64]{1,3,2,0:T(8,128)(2,1)}, pred[2,512]{1,0:T(...) while((s32[]{:T(128)}, bf16[2,512,512]{2,1,0:T(8,128)(2,1)}, ...), condition=%wide.region_3.4_spmd, body=%wide.region_0.3_spmd.sunk | while | flops 562294784 | bytes 33689224 | solution.py:114
  61.3 65.4 %all-reduce.6.cloned.1.call-done = bf16[1024,1024]{1,0:T(8,128)(2,1)} async-done(((bf16[1024,1024]{1,0:T(8,128)(2,1)}), bf16[1024,1024]{1,0:T(8,128)(2,1)}) %all-reduce.6.cloned.1.call-update) | async-done | bytes 2097168 | tf_op jit(solution)/shard_map/psum | solution.py:119
  133.5 24.4 %multiply_convert_fusion.1 = (bf16[1024,2048]{1,0:T(8,128)(2,1)S(1)}, f32[1024,2048]{1,0:T(8,128)}, f32[1024,2048]{1,0:T(8,128)}) fusion(f32[2048]{0:T(1024)S(1)} %convert_element_type.174, bf16[1024,2048]{1,0:T(8,128)(2,1)S(1)} %copy-done.36, f32[1024,1024]{1,0:T(8,128)S(1)} %broadcast_multiply_fusion, f32[1024]{0:T(1024)S(1)} %convert_element_type.172, ...), kind=kOutput, calls=%fused_computation.64 | convolution fusion | flops 4436525056 | bytes 29376512 | tf_op jit(solution)/shard_map/dot_general | solution.py:125
  159.8 5.8 convolution_convert_fusion.3
  166.1 62.6 %all-reduce.8.cloned.1.call-done = bf16[1024,1024]{1,0:T(8,128)(2,1)} async-done(((bf16[1024,1024]{1,0:T(8,128)(2,1)}), bf16[1024,1024]{1,0:T(8,128)(2,1)}) %all-reduce.8.cloned.1.call-update) | async-done | bytes 2097168 | tf_op jit(solution)/shard_map/psum | solution.py:132
  241.1 13.0 %convert_reduce_fusion = (f32[2048]{0:T(1024)}, bf16[1024,2048]{1,0:T(8,128)(2,1)}) fusion(f32[1024,2048]{1,0:T(8,128)} %get-tuple-element.258, bf16[2048,1024]{1,0:T(8,128)(2,1)S(1)} %copy-done.35, f32[1024,1024]{1,0:T(8,128)S(1)} %broadcast_add_fusion.1, f32[1024,2048]{1,0:T(8,128)} %get-tuple-element.275, f32[2048]{0:T(1024)S(1)} %convert_element_type.174), kind=kOutput, calls=%fused_computation.62 | convolution fusion | flops 4331665408 | bytes 29376512 | tf_op jit(solution)/shard_map/dot_general | solution.py:28
  254.1 8.0 convolution_convert_fusion.2
  262.2 56.9 %all-gather.3.cloned.1.call-done = bf16[2048,1024]{1,0:T(8,128)(2,1)} async-done(((bf16[1024,1024]{1,0:T(8,128)(2,1)}), bf16[2048,1024]{1,0:T(8,128)(2,1)}) %all-gather.3.cloned.1.call-update) | async-done | bytes 4194320 | tf_op jit(solution)/shard_map/all_gather | solution.py:149
  319.1 5.2 reduce_sum.205
  324.2 5.7 multiply_reduce_fusion.1
  345.3 42.9 %while.27 = (s32[]{:T(128)}, bf16[2,512,512]{1,2,0:T(8,128)(2,1)}, bf16[2,512,512]{2,1,0:T(8,128)(2,1)}, bf16[2,512,512]{1,2,0:T(8,128)(2,1)}, bf16[2,512,8,64]{...) while((s32[]{:T(128)}, bf16[2,512,512]{1,2,0:T(8,128)(2,1)}, ...), condition=%wide.region_17.18_spmd, body=%wide.region_15.17_spmd.sunk | while | flops 1374941184 | bytes 89248512 | solution.py:162
  392.7 7.7 convert_bitcast_fusion
  400.5 7.7 copy.83
  408.2 4.8 convolution_convert_fusion.5
  413.1 10.2 %convolution_convert_fusion = bf16[2048,1024]{0,1:T(8,128)(2,1)} fusion(bf16[1024,2048]{1,0:T(8,128)(2,1)} %copy-done.40, f32[1024,1024]{1,0:T(8,128)} %copy-done.11), kind=kOutput, calls=%fused_computation.91 | convolution fusion | flops 4298113024 | bytes 12582912 | tf_op jit(solution)/shard_map/dot_general | solution.py:22
  424.0 10.1 %convolution_convert_fusion.1 = bf16[1024,2048]{1,0:T(8,128)(2,1)} fusion(bf16[1024,2048]{1,0:T(8,128)(2,1)} %get-tuple-element.277, f32[1024,1024]{1,0:T(8,128)} %copy-done.7, f32[1024]{0:T(1024)S(1)} %copy-done.25, f32[1024]{0:T(1024)S(1)} %convert_element_type.171), kind=kOutput, calls=%fused_computation.92 | convolution fusion | flops 4300210176 | bytes 12591104 | tf_op jit(solution)/shard_map/dot_general | solution.py:22
  434.2 6.6 bitcast_convert_fusion
  450.7 69.1 %all-reduce.10.cloned.1.call-done = bf16[3,1024,512]{2,0,1:T(4,128)(2,1)} async-done(((bf16[3,1024,512]{2,0,1:T(4,128)(2,1)}), bf16[3,1024,512]{2,0,1:T(4,128)(2,1)}) %all-reduce.10.cloned.1.call-update) | async-done | bytes 3145744
  521.6 58.4 %reduce-scatter.7.cloned.1.call-done = bf16[512,64]{0,1:T(8,128)(2,1)} async-done(((bf16[512,1024]{0,1:T(8,128)(2,1)}), bf16[512,64]{0,1:T(8,128)(2,1)}) %reduce-scatter.7.cloned.1.call-update) | async-done | bytes 65552 | tf_op jit(solution)/shard_map/reduce_scatter | solution.py:187
  581.5 73.9 %reduce-scatter.11.cloned.1.call-done = bf16[2048,64]{0,1:T(8,128)(2,1)} async-done(((bf16[2048,1024]{0,1:T(8,128)(2,1)}), bf16[2048,64]{0,1:T(8,128)(2,1)}) %reduce-scatter.11.cloned.1.call-update) | async-done | bytes 262160 | tf_op jit(solution)/shard_map/reduce_scatter | solution.py:193
  657.3 74.0 %reduce-scatter.9.cloned.1.call-done = bf16[64,2048]{1,0:T(8,128)(2,1)} async-done(((bf16[1024,2048]{1,0:T(8,128)(2,1)}), bf16[64,2048]{1,0:T(8,128)(2,1)}) %reduce-scatter.9.cloned.1.call-update) | async-done | bytes 262160 | tf_op jit(solution)/shard_map/reduce_scatter | solution.py:190
  733.0 31.4 %reduce-scatter.5.cloned.1.call-done = bf16[512,1024]{1,0:T(8,128)(2,1)} async-done(((bf16[1024,1024]{1,0:T(8,128)(2,1)}), bf16[512,1024]{1,0:T(8,128)(2,1)}) %reduce-scatter.5.cloned.1.call-update) | async-done | bytes 1048592 | tf_op jit(solution)/shard_map/reduce_scatter | solution.py:181
  767.7 40.7 %all-reduce.1 = (f32[2,1024]{1,0:T(2,128)}, f32[1024]{0:T(1024)}, f32[1024]{0:T(1024)}, f32[1024]{0:T(1024)}, f32[4096]{0:T(1024)}, /*index=5*/f32[1024]{0:T(1024)}, f32[1024]{0:T(1024)}, f32[1024]{0:T(1024)}) all-reduce(f32[2,1024]{1,0:T(2,128)S(1)} %maximum_dynamic-update-slice_fusion, ...), channel_id=1, replica_groups=mesh['dp'=16,'mp'=2] {'dp','mp'}, use_global_device_ids=true, to_apply=%region_22.23 | all-reduce | flops 12288 | bytes 98304 | tf_op jit(solution)/shard_map/psum | solution.py:203
  (205 shorter events, 152.3 us)
Async XLA Ops:
  7.2 119.5 %all-reduce.6.cloned.1.call-start = ((), (), s32[]{:S(2)}) async-start(), calls=%async_computation.4 | async-start | bytes 4194304 | tf_op jit(solution)/shard_map/psum | solution.py:119
  60.9 167.8 %all-reduce.8.cloned.1.call-start = ((), (), s32[]{:S(2)}) async-start(), calls=%async_computation.5 | async-start | bytes 4194304 | tf_op jit(solution)/shard_map/psum | solution.py:132
  61.3 171.3 %copy-start.24 = (f32[1024]{0:T(1024)}, f32[1024]{0:T(1024)S(1)}, u32[]{:S(2)}) copy-start(f32[1024]{0:T(1024)S(1)} %convert_element_type.172) | copy-start | bytes 12292
  133.4 24.4 %copy-start.7 = (f32[1024,1024]{1,0:T(8,128)}, f32[1024,1024]{1,0:T(8,128)S(1)}, u32[]{:S(2)}) copy-start(f32[1024,1024]{1,0:T(8,128)S(1)} %broadcast_multiply_fusion) | copy-start | bytes 12582916
  133.5 26.4 %copy-start.34 = (bf16[2048,1024]{1,0:T(8,128)(2,1)S(1)}, bf16[2048,1024]{1,0:T(8,128)(2,1)}, u32[]{:S(2)}) copy-start(bf16[2048,1024]{1,0:T(8,128)(2,1)} %param.29) | copy-start | bytes 12582916
  159.8 6.3 copy-start.31
  159.8 6.3 copy-start.32
  165.6 153.4 %all-gather.3.cloned.1.call-start = ((), (), s32[]{:S(2)}) async-start(), calls=%async_computation.10 | async-start | bytes 6291456 | tf_op jit(solution)/shard_map/all_gather | solution.py:149
  166.1 72.0 %copy-start.20 = (f32[1024]{0:T(1024)}, f32[1024]{0:T(1024)S(1)}, u32[]{:S(2)}) copy-start(f32[1024]{0:T(1024)S(1)} %convert_element_type.179) | copy-start | bytes 12292
  239.4 14.7 %copy-start.11 = (f32[1024,1024]{1,0:T(8,128)}, f32[1024,1024]{1,0:T(8,128)S(1)}, u32[]{:S(2)}) copy-start(f32[1024,1024]{1,0:T(8,128)S(1)} %broadcast_add_fusion.1) | copy-start | bytes 12582916
  241.1 13.0 %copy-start.37 = (bf16[1024,2048]{1,0:T(8,128)(2,1)S(1)}, bf16[1024,2048]{1,0:T(8,128)(2,1)}, u32[]{:S(2)}) copy-start(bf16[1024,2048]{1,0:T(8,128)(2,1)} %param.27) | copy-start | bytes 12582916
  262.1 257.7 %all-reduce.10.cloned.1.call-start = ((), (), s32[]{:S(2)}) async-start(), calls=%async_computation.11 | async-start | bytes 8388608
  324.2 5.8 copy-start.4
  324.2 5.8 copy-start.6
  408.2 171.9 %reduce-scatter.7.cloned.1.call-start = ((), (), s32[]{:S(2)}) async-start(), calls=%async_computation.7 | async-start | bytes 1114112 | tf_op jit(solution)/shard_map/reduce_scatter | solution.py:187
  413.0 242.4 %reduce-scatter.11.cloned.1.call-start = ((), (), s32[]{:S(2)}) async-start(), calls=%async_computation.9 | async-start | bytes 4456448 | tf_op jit(solution)/shard_map/reduce_scatter | solution.py:193
  423.3 307.9 %reduce-scatter.9.cloned.1.call-start = ((), (), s32[]{:S(2)}) async-start(), calls=%async_computation.8 | async-start | bytes 4456448 | tf_op jit(solution)/shard_map/reduce_scatter | solution.py:190
  434.2 6.8 copy-start.33
  434.2 6.8 copy-start.39
  434.2 8.0 copy-start.23
  434.2 8.1 copy-start.26
  434.2 330.3 %reduce-scatter.5.cloned.1.call-start = ((), (), s32[]{:S(2)}) async-start(), calls=%async_computation.6 | async-start | bytes 3145728 | tf_op jit(solution)/shard_map/reduce_scatter | solution.py:181
  442.2 6.0 copy-start.9
  444.6 5.7 copy-start.18
  (30 other events, 89.3 us)
Sparse Core Ops, SparseCore 0:
  61.1 65.5 all-reduce.5
  165.8 62.9 all-reduce.7
  262.3 56.7 all-gather.2
  408.3 111.4 all-reduce.9
  523.7 56.3 reduce-scatter.6
  583.8 71.6 reduce-scatter.10
  659.8 71.3 reduce-scatter.8
  733.5 30.9 reduce-scatter.4
